TPU v7x, 32 devices: a whole 2x2x4 slice. The times are simulated.
32 devices in a mesh: days: 2 (over x), tm: 8 (over z, y), sta: 2 (over core).
Axes of the slice: x: 2, y: 2, z: 4, core: 2. Of those that a mesh axis runs over, the one named last changes fastest.
Arguments:
- records: bfloat16 [2048, 2048], P('sta', ('days', 'tm')), parts along dimension 1, may hold values from -6 to 6
- following: bfloat16 [2048, 510], P('sta', 'days'), parts along dimension 1, may hold values from -6 to 6
- library: bfloat16 [32, 2048, 256], P(None, ('sta', 'tm')), may hold values from -6 to 6
- template_ids: int32 [2, 8], replicated, may hold values from 0 to 31
- channel_mask: int32 [32, 2048], replicated, may hold values 0 or 1
- station_group: int32 [2048], replicated, may hold values from 0 to 127
Outputs:
- detection: float32 [2, 8, 2048], P('sta', None, ('days', 'tm')), parts along dimension 2
There are 2 independent parts, one for each index of `days`. A program takes and returns all parts, laid end to end along the dimension named above; an argument that names none is the same for every part. Nothing has to cross between parts.
All inputs are finite; a program needn't handle non-finite values.
Results may differ from a plain program's by a relative error of at most 0.0003.
Values may be sent and summed in bfloat16 or wider, within the bound.
A program may use at most 128 MiB of HBM per device.

v0:
```python
import jax
import jax.numpy as jnp
from jax import lax
from jax.sharding import PartitionSpec as P

W = 256
NB = 2
KB = 8
G = 128
epsilon = 1e-06


def inverse_norm(stream_rows, out_len):
    squares = jnp.square(stream_rows.astype(jnp.float32))
    running = jnp.cumsum(squares, axis=1)
    running = jnp.concatenate([jnp.zeros((running.shape[0], 1), jnp.float32), running], axis=1)
    energy = (running[:, W : W + out_len] - running[:, :out_len]) / W
    return 1.0 / jnp.sqrt(energy + epsilon)


def correlate(rows, temp_rows, out_len):
    block_size = rows.shape[0]
    slot_count = temp_rows.shape[0]
    kernel = jnp.transpose(temp_rows, (1, 0, 2)).reshape(block_size * slot_count, 1, W)
    result = lax.conv_general_dilated(
        rows[None],
        kernel,
        (1,),
        "VALID",
        dimension_numbers=("NCH", "OIH", "NCH"),
        feature_group_count=block_size,
        preferred_element_type=jnp.float32,
    )
    return result[0, :, :out_len].reshape(block_size, slot_count, out_len)


def station_terms(stream_rows, temps, weights, inverse):
    station_count = stream_rows.shape[0]
    out_len = inverse.shape[1]
    slot_count = temps.shape[0]
    size_limit = max(1, (1 << 22) // (W * out_len))
    block_size = max(
        (
            divisor
            for divisor in range(1, station_count + 1)
            if station_count % divisor == 0 and divisor <= size_limit
        )
    )
    turn_count = station_count // block_size
    rows_blocks = stream_rows.reshape(turn_count, block_size, stream_rows.shape[1])
    temp_blocks = jnp.moveaxis(temps.reshape(slot_count, turn_count, block_size, W), 1, 0)
    weight_blocks = jnp.moveaxis(weights.reshape(slot_count, turn_count, block_size), 1, 0)
    scale_blocks = inverse.reshape(turn_count, block_size, out_len)

    def advance(running, inputs):
        rows, temp_rows, weight, scale = inputs
        corr = correlate(rows, temp_rows, out_len)
        factor = jnp.transpose(weight)[:, :, None] * scale[:, None, :]
        return (running + jnp.sum(corr * factor, axis=0), None)

    start_zero = jnp.zeros((slot_count, out_len), jnp.float32)
    return lax.scan(advance, start_zero, (rows_blocks, temp_blocks, weight_blocks, scale_blocks))[0]


def shards(records, following, library, template_ids, channel_mask, station_group):
    sta_rows = records.shape[0]
    block_len = records.shape[1]
    sub_rows = library.shape[1]
    base = lax.axis_index("sta") * sta_rows
    onehot = (station_group[:, None] == jnp.arange(G, dtype=jnp.int32)[None, :]).astype(jnp.int32)
    counts = jnp.dot(channel_mask, onehot, preferred_element_type=jnp.int32)
    my_mask = lax.dynamic_slice_in_dim(channel_mask, base, sta_rows, 1)
    my_group = lax.dynamic_slice_in_dim(station_group, base, sta_rows, 0)
    per_station = jnp.take(counts, my_group, axis=1)
    scaled = my_mask.astype(jnp.float32) / jnp.sqrt(
        jnp.float32(W * G) * jnp.maximum(per_station, 1).astype(jnp.float32)
    )
    flat_ids = template_ids.reshape(-1)
    position = lax.axis_index("tm")
    moved = lax.all_to_all(records, "tm", split_axis=0, concat_axis=1, tiled=True)
    offset = position * sub_rows
    tail_rows = lax.dynamic_slice_in_dim(following, offset, sub_rows, 0)
    stream = jnp.concatenate([moved, tail_rows], axis=1)
    inverse = inverse_norm(stream, moved.shape[1])
    tmean = jnp.mean(jnp.square(library.astype(jnp.float32)), axis=2)
    factor = lax.dynamic_slice_in_dim(scaled, offset, sub_rows, 1) / jnp.sqrt(tmean + epsilon)
    chosen = jnp.take(library, flat_ids, axis=0)
    weights = jnp.take(factor, flat_ids, axis=0)
    partial_sum = station_terms(stream, chosen, weights, inverse)
    totals = lax.psum_scatter(partial_sum, "tm", scatter_dimension=1, tiled=True)
    return lax.psum_scatter(
        totals.reshape(NB, KB, block_len), "sta", scatter_dimension=0, tiled=True
    )


def solution(mesh):
    placed = (
        P("sta", ("days", "tm")),
        P("sta", "days"),
        P(None, ("sta", "tm"), None),
        P(),
        P(),
        P(),
    )
    return jax.shard_map(
        shards,
        mesh=mesh,
        in_specs=placed,
        out_specs=P("sta", None, ("days", "tm")),
        check_vma=False,
    )
```

profile of v0, /device:TPU:0, one launch (start us, length us, event | category | flops | bytes accessed | tf_op | source)
XLA Modules:
  0.0 272.6 jit_solution(17316995010624979843)
XLA Ops:
  6.5 7.6 %all-to-all-start = ((bf16[8,128,128]{2,1,0:T(8,128)(2,1)}), bf16[8,128,128]{2,1,0:T(8,128)(2,1)S(1)}, u32[]{:S(2)}, u32[]{:S(2)}) async-start(bf16[8,128,128]{2,1,0:T(8,128)(2,1)} %bitcast.60), calls=%async_computation | async-start | bytes 524288 | tf_op jit(solution)/shard_map/all_to_all | solution.py:80
  17.8 1.6 convolution_bitcast_fusion
  19.5 2.8 %gather_fusion.1 = s32[1024,32]{1,0:T(8,128)S(1)} fusion(s32[32,128]{0,1:T(8,128)S(1)} %copy.46, s32[1024]{0:T(1024)S(1)} %fusion.14), kind=kCustom, calls=%fused_computation.1 | custom fusion | bytes 266240 | tf_op jit(solution)/shard_map/jit(_take)/gather | solution.py:74
  23.8 1.6 gather_fusion
  27.0 2.4 select_bitcast_fusion
  32.0 173.0 %while.11 = (s32[]{:T(128)}, f32[16,1024]{1,0:T(8,128)S(1)}, bf16[8,16,1279]{2,1,0:T(8,128)(2,1)}, bf16[8,16,16,256]{3,2,0,1:T(8,128)(2,1)}, f32[8,16,16]{1,2,0:...) while((s32[]{:T(128)}, f32[16,1024]{1,0:T(8,128)S(1)}, ...), condition=%wide.region_5.6_spmd.clone, body=%wide.region_3.5_spmd.clone.sunk | while | flops 2150383616 | bytes 5779415 | solution.py:62
  33.5 0.9 constant_dynamic-slice_fusion.7
  34.6 17.5 %fusion.23 = f32[1,256,1024]{1,0,2:T(1,128)S(1)} fusion(bf16[1,16,1279]{1,0,2:T(2,128)(2,1)S(1)} %copy.65, s32[256]{0:T(256)S(1)} %get-tuple-element.151, bf16[256,256]{0,1:T(8,128)(2,1)S(1)} %copy.67), kind=kOutput, calls=%fused_computation.5.clone.1 | convolution fusion | flops 2149580800 | bytes 1221600 | tf_op jit(solution)/shard_map/while/body/eval_jaxpr/conv_general_dilated | solution.py:25
  52.0 1.3 copy.68
  55.1 0.9 constant_dynamic-slice_fusion.7
  56.2 17.5 %fusion.23 = f32[1,256,1024]{1,0,2:T(1,128)S(1)} fusion(bf16[1,16,1279]{1,0,2:T(2,128)(2,1)S(1)} %copy.65, s32[256]{0:T(256)S(1)} %get-tuple-element.151, bf16[256,256]{0,1:T(8,128)(2,1)S(1)} %copy.67), kind=kOutput, calls=%fused_computation.5.clone.1 | convolution fusion | flops 2149580800 | bytes 1221600 | tf_op jit(solution)/shard_map/while/body/eval_jaxpr/conv_general_dilated | solution.py:25
  73.7 1.3 copy.68
  76.7 0.9 constant_dynamic-slice_fusion.7
  77.8 17.5 %fusion.23 = f32[1,256,1024]{1,0,2:T(1,128)S(1)} fusion(bf16[1,16,1279]{1,0,2:T(2,128)(2,1)S(1)} %copy.65, s32[256]{0:T(256)S(1)} %get-tuple-element.151, bf16[256,256]{0,1:T(8,128)(2,1)S(1)} %copy.67), kind=kOutput, calls=%fused_computation.5.clone.1 | convolution fusion | flops 2149580800 | bytes 1221600 | tf_op jit(solution)/shard_map/while/body/eval_jaxpr/conv_general_dilated | solution.py:25
  95.3 1.3 copy.68
  98.4 0.9 constant_dynamic-slice_fusion.7
  99.4 17.5 %fusion.23 = f32[1,256,1024]{1,0,2:T(1,128)S(1)} fusion(bf16[1,16,1279]{1,0,2:T(2,128)(2,1)S(1)} %copy.65, s32[256]{0:T(256)S(1)} %get-tuple-element.151, bf16[256,256]{0,1:T(8,128)(2,1)S(1)} %copy.67), kind=kOutput, calls=%fused_computation.5.clone.1 | convolution fusion | flops 2149580800 | bytes 1221600 | tf_op jit(solution)/shard_map/while/body/eval_jaxpr/conv_general_dilated | solution.py:25
  116.9 1.3 copy.68
  121.1 17.5 %fusion.23 = f32[1,256,1024]{1,0,2:T(1,128)S(1)} fusion(bf16[1,16,1279]{1,0,2:T(2,128)(2,1)S(1)} %copy.65, s32[256]{0:T(256)S(1)} %get-tuple-element.151, bf16[256,256]{0,1:T(8,128)(2,1)S(1)} %copy.67), kind=kOutput, calls=%fused_computation.5.clone.1 | convolution fusion | flops 2149580800 | bytes 1221600 | tf_op jit(solution)/shard_map/while/body/eval_jaxpr/conv_general_dilated | solution.py:25
  138.5 1.3 copy.68
  141.6 0.9 constant_dynamic-slice_fusion.7
  142.7 17.5 %fusion.23 = f32[1,256,1024]{1,0,2:T(1,128)S(1)} fusion(bf16[1,16,1279]{1,0,2:T(2,128)(2,1)S(1)} %copy.65, s32[256]{0:T(256)S(1)} %get-tuple-element.151, bf16[256,256]{0,1:T(8,128)(2,1)S(1)} %copy.67), kind=kOutput, calls=%fused_computation.5.clone.1 | convolution fusion | flops 2149580800 | bytes 1221600 | tf_op jit(solution)/shard_map/while/body/eval_jaxpr/conv_general_dilated | solution.py:25
  160.1 1.3 copy.68
  163.2 0.9 constant_dynamic-slice_fusion.7
  164.3 17.5 %fusion.23 = f32[1,256,1024]{1,0,2:T(1,128)S(1)} fusion(bf16[1,16,1279]{1,0,2:T(2,128)(2,1)S(1)} %copy.65, s32[256]{0:T(256)S(1)} %get-tuple-element.151, bf16[256,256]{0,1:T(8,128)(2,1)S(1)} %copy.67), kind=kOutput, calls=%fused_computation.5.clone.1 | convolution fusion | flops 2149580800 | bytes 1221600 | tf_op jit(solution)/shard_map/while/body/eval_jaxpr/conv_general_dilated | solution.py:25
  181.8 1.3 copy.68
  184.8 0.9 constant_dynamic-slice_fusion.7
  185.9 17.5 %fusion.23 = f32[1,256,1024]{1,0,2:T(1,128)S(1)} fusion(bf16[1,16,1279]{1,0,2:T(2,128)(2,1)S(1)} %copy.65, s32[256]{0:T(256)S(1)} %get-tuple-element.151, bf16[256,256]{0,1:T(8,128)(2,1)S(1)} %copy.67), kind=kOutput, calls=%fused_computation.5.clone.1 | convolution fusion | flops 2149580800 | bytes 1221600 | tf_op jit(solution)/shard_map/while/body/eval_jaxpr/conv_general_dilated | solution.py:25
  203.4 1.3 copy.68
  206.2 55.7 %reduce-scatter.2.cloned.1.call-done = f32[16,128]{1,0:T(8,128)} async-done(((f32[16,1024]{1,0:T(8,128)}), f32[16,128]{1,0:T(8,128)}) %reduce-scatter.2.cloned.1.call-update) | async-done | bytes 8208 | tf_op jit(solution)/shard_map/reduce_scatter | solution.py:90
  262.0 2.6 all-reduce.2
  264.6 1.2 constant_dynamic-slice_fusion.3
  (118 shorter events, 26.1 us)
Async XLA Ops:
  6.5 10.5 %copy-start = (bf16[1024,255]{1,0:T(8,128)(2,1)S(1)}, bf16[1024,255]{1,0:T(8,128)(2,1)}, u32[]{:S(2)}) copy-start(bf16[1024,255]{1,0:T(8,128)(2,1)} %param.9) | copy-start | bytes 1566724
  6.5 16.6 %copy-start.1 = (bf16[32,128,256]{2,1,0:T(8,128)(2,1)S(1)}, bf16[32,128,256]{2,1,0:T(8,128)(2,1)}, u32[]{:S(2)}) copy-start(bf16[32,128,256]{2,1,0:T(8,128)(2,1)} %param.10) | copy-start | bytes 6291460
  6.5 22.8 %all-to-all-start = ((bf16[8,128,128]{2,1,0:T(8,128)(2,1)}), bf16[8,128,128]{2,1,0:T(8,128)(2,1)S(1)}, u32[]{:S(2)}, u32[]{:S(2)}) async-start(bf16[8,128,128]{2,1,0:T(8,128)(2,1)} %bitcast.60), calls=%async_computation | async-start | bytes 524288 | tf_op jit(solution)/shard_map/all_to_all | solution.py:80
  14.1 247.9 %reduce-scatter.2.cloned.1.call-start = ((), (), s32[]{:S(2)}) async-start(), calls=%async_computation.2 | async-start | bytes 73728 | tf_op jit(solution)/shard_map/reduce_scatter | solution.py:90
  17.1 0.7 copy-start.3
  23.2 2.3 copy-start.5
  25.5 4.2 %copy-start.6 = (bf16[128,255]{0,1:T(8,128)(2,1)S(1)}, bf16[128,255]{0,1:T(8,128)(2,1)}, u32[]{:S(2)}) copy-start(bf16[128,255]{0,1:T(8,128)(2,1)} %copy.50) | copy-start | bytes 195844
  30.4 0.8 copy-start.4
  30.6 1.4 copy-start.8
  32.0 173.6 %copy-start.7 = (u32[32]{0:T(128)S(1)}, u32[32]{0:T(128)}, u32[]{:S(2)}) copy-start(u32[32]{0:T(128)} %constant.105) | copy-start | bytes 388
  205.0 0.6 copy-start.2
Sparse Core Ops, SparseCore 0:
  205.7 56.1 reduce-scatter.1
where the time goes:
time: 274 us; the launch traced here: 273 us
  matrix products  141 us (51%)
  waiting for transfers between devices  55.8 us (20%)
  local copies, waits for them, and re-layouts  42.9 us (16%)
  between operations  13.6 us (5%)
  other arithmetic  8.16 us (3%)
  starting transfers between devices  7.61 us (3%)
    conv_general_dilated x8, matrix products, correlate(): lax.conv_general_dilated(rows[None], kernel, (1,), 'VALID', dimension_num...  140 us
    reduce_scatter x1, waiting for transfers between devices, shards(): lax.psum_scatter(partial_sum, 'tm', scatter_dimension=1, tiled=True)  55.7 us
    dynamic_slice x32, local copies, waits for them, and re-layouts, station_terms(): lax.scan(advance, start_zero, (rows_blocks, temp_blocks, weight_blocks, s...  19.6 us
    conv_general_dilated x8, local copies, waits for them, and re-layouts, correlate(): lax.conv_general_dilated(rows[None], kernel, (1,), 'VALID', dimension_num...  10.6 us
    all_to_all x1, starting transfers between devices, shards(): lax.all_to_all(records, 'tm', split_axis=0, concat_axis=1, tiled=True)  7.57 us
  transfers between devices with their start and end apart: 2, of which 1 were waited for; matrix products, arithmetic and copies ran while one was open for 6% of the time, Pallas kernels for 0%

commit v1 on v0

--- a/solution.py
+++ b/solution.py
@@ -77,7 +77,11 @@
     )
     flat_ids = template_ids.reshape(-1)
     position = lax.axis_index("tm")
-    moved = lax.all_to_all(records, "tm", split_axis=0, concat_axis=1, tiled=True)
+    n_now = lax.axis_size("tm")
+    small = jnp.split(records, n_now, 0)
+    later = jnp.stack(small)
+    a_next = lax.all_to_all(later, axis_name="tm", split_axis=0, concat_axis=0)
+    moved = jnp.concatenate(a_next, 1)
     offset = position * sub_rows
     tail_rows = lax.dynamic_slice_in_dim(following, offset, sub_rows, 0)
     stream = jnp.concatenate([moved, tail_rows], axis=1)

time: 274 us -> 283 us (1.033)
  local copies, waits for them, and re-layouts: 42.9 us -> 53.8 us
    transpose x8, local copies, waits for them, and re-layouts: 0.08 us -> 5.64 us  [advance(): factor = jnp.transpose(weight)[:, :, None] * scale[:, None, :]]
    unnamed x20 -> x41, local copies, waits for them, and re-layouts: 2.57 us -> 7.8 us
  transfers between devices with their start and end apart: 2 -> 2, of which waited for: 1 -> 1; matrix products, arithmetic and copies ran while one was open for 6% -> 4% of each run, Pallas kernels for 0% -> 0%
where the time goes in v1:
time: 283 us; the launch traced here: 281 us
  matrix products  140 us (49%)
  waiting for transfers between devices  55.8 us (20%)
  local copies, waits for them, and re-layouts  53.8 us (19%)
  between operations  13.7 us (5%)
  other arithmetic  7.38 us (3%)
  starting transfers between devices  7.35 us (3%)
    conv_general_dilated x8, matrix products, correlate(): lax.conv_general_dilated(rows[None], kernel, (1,), 'VALID', dimension_num...  140 us
    reduce_scatter x1, waiting for transfers between devices, shards(): lax.psum_scatter(partial_sum, 'tm', scatter_dimension=1, tiled=True)  55.8 us
    dynamic_slice x32, local copies, waits for them, and re-layouts, station_terms(): lax.scan(advance, start_zero, (rows_blocks, temp_blocks, weight_blocks, s...  19.6 us
    conv_general_dilated x8, local copies, waits for them, and re-layouts, correlate(): lax.conv_general_dilated(rows[None], kernel, (1,), 'VALID', dimension_num...  10.6 us
    unnamed x41, local copies, waits for them, and re-layouts  7.8 us
    all_to_all x1, starting transfers between devices, shards(): a_next = lax.all_to_all(later, axis_name='tm', split_axis=0, concat_axis=0)  7.31 us
  transfers between devices with their start and end apart: 2, of which 1 were waited for; matrix products, arithmetic and copies ran while one was open for 4% of the time, Pallas kernels for 0%

profile of v1, /device:TPU:0, one launch (start us, length us, event | category | flops | bytes accessed | tf_op | source)
XLA Modules:
  0.0 281.5 jit_solution(10748305741971988603)
XLA Ops:
  6.5 1.0 fusion.16
  13.4 7.3 %all-to-all-start = ((bf16[8,128,128]{1,2,0:T(8,128)(2,1)}), bf16[8,128,128]{1,2,0:T(8,128)(2,1)S(1)}, u32[]{:S(2)}, u32[]{:S(2)}) async-start(bf16[8,128,128]{1,2,0:T(8,128)(2,1)} %bitcast_dynamic-update-slice_fusion), calls=%async_computation | async-start | bytes 524288 | tf_op jit(solution)/shard_map/all_to_all | solution.py:83
  22.6 2.8 gather_fusion.1
  26.9 1.6 gather_fusion
  30.6 2.4 select_bitcast_fusion
  35.4 178.5 %while.11 = (s32[]{:T(128)}, f32[16,1024]{1,0:T(8,128)S(1)}, bf16[8,16,1279]{2,1,0:T(8,128)(2,1)}, bf16[8,16,16,256]{3,2,0,1:T(8,128)(2,1)}, f32[8,16,16]{1,2,0:...) while((s32[]{:T(128)}, f32[16,1024]{1,0:T(8,128)S(1)}, ...), condition=%wide.region_5.6_spmd.clone, body=%wide.region_3.5_spmd.clone.sunk | while | flops 2150383616 | bytes 5779415 | solution.py:62
  36.9 0.9 constant_dynamic-slice_fusion.7
  38.0 17.5 %fusion.24 = f32[1,256,1024]{1,0,2:T(1,128)S(1)} fusion(bf16[1,16,1279]{1,0,2:T(2,128)(2,1)S(1)} %copy.93, s32[256]{0:T(256)S(1)} %get-tuple-element.161, bf16[256,256]{0,1:T(8,128)(2,1)S(1)} %copy.95), kind=kOutput, calls=%fused_computation.5.clone.1 | convolution fusion | flops 2149580800 | bytes 1221600 | tf_op jit(solution)/shard_map/while/body/eval_jaxpr/conv_general_dilated | solution.py:25
  55.5 1.3 copy.96
  59.2 0.9 constant_dynamic-slice_fusion.7
  60.3 17.5 %fusion.24 = f32[1,256,1024]{1,0,2:T(1,128)S(1)} fusion(bf16[1,16,1279]{1,0,2:T(2,128)(2,1)S(1)} %copy.93, s32[256]{0:T(256)S(1)} %get-tuple-element.161, bf16[256,256]{0,1:T(8,128)(2,1)S(1)} %copy.95), kind=kOutput, calls=%fused_computation.5.clone.1 | convolution fusion | flops 2149580800 | bytes 1221600 | tf_op jit(solution)/shard_map/while/body/eval_jaxpr/conv_general_dilated | solution.py:25
  77.8 1.3 copy.96
  81.5 0.9 constant_dynamic-slice_fusion.7
  82.6 17.5 %fusion.24 = f32[1,256,1024]{1,0,2:T(1,128)S(1)} fusion(bf16[1,16,1279]{1,0,2:T(2,128)(2,1)S(1)} %copy.93, s32[256]{0:T(256)S(1)} %get-tuple-element.161, bf16[256,256]{0,1:T(8,128)(2,1)S(1)} %copy.95), kind=kOutput, calls=%fused_computation.5.clone.1 | convolution fusion | flops 2149580800 | bytes 1221600 | tf_op jit(solution)/shard_map/while/body/eval_jaxpr/conv_general_dilated | solution.py:25
  100.1 1.3 copy.96
  103.8 0.9 constant_dynamic-slice_fusion.7
  104.9 17.5 %fusion.24 = f32[1,256,1024]{1,0,2:T(1,128)S(1)} fusion(bf16[1,16,1279]{1,0,2:T(2,128)(2,1)S(1)} %copy.93, s32[256]{0:T(256)S(1)} %get-tuple-element.161, bf16[256,256]{0,1:T(8,128)(2,1)S(1)} %copy.95), kind=kOutput, calls=%fused_computation.5.clone.1 | convolution fusion | flops 2149580800 | bytes 1221600 | tf_op jit(solution)/shard_map/while/body/eval_jaxpr/conv_general_dilated | solution.py:25
  122.4 1.3 copy.96
  126.2 0.9 constant_dynamic-slice_fusion.7
  127.2 17.5 %fusion.24 = f32[1,256,1024]{1,0,2:T(1,128)S(1)} fusion(bf16[1,16,1279]{1,0,2:T(2,128)(2,1)S(1)} %copy.93, s32[256]{0:T(256)S(1)} %get-tuple-element.161, bf16[256,256]{0,1:T(8,128)(2,1)S(1)} %copy.95), kind=kOutput, calls=%fused_computation.5.clone.1 | convolution fusion | flops 2149580800 | bytes 1221600 | tf_op jit(solution)/shard_map/while/body/eval_jaxpr/conv_general_dilated | solution.py:25
  144.7 1.3 copy.96
  149.6 17.5 %fusion.24 = f32[1,256,1024]{1,0,2:T(1,128)S(1)} fusion(bf16[1,16,1279]{1,0,2:T(2,128)(2,1)S(1)} %copy.93, s32[256]{0:T(256)S(1)} %get-tuple-element.161, bf16[256,256]{0,1:T(8,128)(2,1)S(1)} %copy.95), kind=kOutput, calls=%fused_computation.5.clone.1 | convolution fusion | flops 2149580800 | bytes 1221600 | tf_op jit(solution)/shard_map/while/body/eval_jaxpr/conv_general_dilated | solution.py:25
  167.0 1.3 copy.96
  170.8 0.9 constant_dynamic-slice_fusion.7
  171.9 17.5 %fusion.24 = f32[1,256,1024]{1,0,2:T(1,128)S(1)} fusion(bf16[1,16,1279]{1,0,2:T(2,128)(2,1)S(1)} %copy.93, s32[256]{0:T(256)S(1)} %get-tuple-element.161, bf16[256,256]{0,1:T(8,128)(2,1)S(1)} %copy.95), kind=kOutput, calls=%fused_computation.5.clone.1 | convolution fusion | flops 2149580800 | bytes 1221600 | tf_op jit(solution)/shard_map/while/body/eval_jaxpr/conv_general_dilated | solution.py:25
  189.3 1.3 copy.96
  193.1 0.9 constant_dynamic-slice_fusion.7
  194.2 17.5 %fusion.24 = f32[1,256,1024]{1,0,2:T(1,128)S(1)} fusion(bf16[1,16,1279]{1,0,2:T(2,128)(2,1)S(1)} %copy.93, s32[256]{0:T(256)S(1)} %get-tuple-element.161, bf16[256,256]{0,1:T(8,128)(2,1)S(1)} %copy.95), kind=kOutput, calls=%fused_computation.5.clone.1 | convolution fusion | flops 2149580800 | bytes 1221600 | tf_op jit(solution)/shard_map/while/body/eval_jaxpr/conv_general_dilated | solution.py:25
  211.6 1.3 copy.96
  215.1 55.8 %reduce-scatter.2.cloned.1.call-done = f32[16,128]{1,0:T(8,128)} async-done(((f32[16,1024]{1,0:T(8,128)}), f32[16,128]{1,0:T(8,128)}) %reduce-scatter.2.cloned.1.call-update) | async-done | bytes 8208 | tf_op jit(solution)/shard_map/reduce_scatter | solution.py:94
  270.9 2.6 all-reduce.2
  273.5 1.2 constant_dynamic-slice_fusion.3
  (139 shorter events, 35.9 us)
Async XLA Ops:
  6.5 14.4 %copy-start = (bf16[1024,255]{1,0:T(8,128)(2,1)S(1)}, bf16[1024,255]{1,0:T(8,128)(2,1)}, u32[]{:S(2)}) copy-start(bf16[1024,255]{1,0:T(8,128)(2,1)} %param.9) | copy-start | bytes 1566724
  6.5 14.3 %copy-start.9 = (s32[2,8]{1,0:T(2,128)S(1)}, s32[2,8]{1,0:T(2,128)}, u32[]{:S(2)}) copy-start(s32[2,8]{1,0:T(2,128)} %param.11) | copy-start | bytes 196
  6.5 15.2 %copy-start.7 = (s32[2048]{0:T(1024)S(1)}, s32[2048]{0:T(1024)}, u32[]{:S(2)}) copy-start(s32[2048]{0:T(1024)} %param.13) | copy-start | bytes 24580
  6.5 15.2 %copy-start.8 = (s32[32,2048]{1,0:T(8,128)S(1)}, s32[32,2048]{1,0:T(8,128)}, u32[]{:S(2)}) copy-start(s32[32,2048]{1,0:T(8,128)} %param.12) | copy-start | bytes 786436
  7.5 18.7 %copy-start.1 = (bf16[32,128,256]{2,1,0:T(8,128)(2,1)S(1)}, bf16[32,128,256]{2,1,0:T(8,128)(2,1)}, u32[]{:S(2)}) copy-start(bf16[32,128,256]{2,1,0:T(8,128)(2,1)} %param.10) | copy-start | bytes 6291460
  13.4 19.5 %all-to-all-start = ((bf16[8,128,128]{1,2,0:T(8,128)(2,1)}), bf16[8,128,128]{1,2,0:T(8,128)(2,1)S(1)}, u32[]{:S(2)}, u32[]{:S(2)}) async-start(bf16[8,128,128]{1,2,0:T(8,128)(2,1)} %bitcast_dynamic-update-slice_fusion), calls=%async_computation | async-start | bytes 524288 | tf_op jit(solution)/shard_map/all_to_all | solution.py:83
  20.8 250.1 %reduce-scatter.2.cloned.1.call-start = ((), (), s32[]{:S(2)}) async-start(), calls=%async_computation.2 | async-start | bytes 73728 | tf_op jit(solution)/shard_map/reduce_scatter | solution.py:94
  21.0 0.8 copy-start.3
  26.2 2.3 copy-start.5
  26.8 6.1 %copy-start.6 = (bf16[128,255]{0,1:T(8,128)(2,1)S(1)}, bf16[128,255]{0,1:T(8,128)(2,1)}, u32[]{:S(2)}) copy-start(bf16[128,255]{0,1:T(8,128)(2,1)} %copy.70) | copy-start | bytes 195844
  33.8 0.8 copy-start.4
  33.8 1.6 copy-start.11
  35.4 179.1 %copy-start.10 = (u32[32]{0:T(128)S(1)}, u32[32]{0:T(128)}, u32[]{:S(2)}) copy-start(u32[32]{0:T(128)} %constant.105) | copy-start | bytes 388
  213.9 0.6 copy-start.2
Sparse Core Ops, SparseCore 0:
  214.7 56.1 reduce-scatter.1
